TPU v7x, 32 devices: a whole 2x2x4 slice. The times are simulated.
32 devices in a mesh: groups: 2 (over x), row: 16 (over z, y, core).
Axes of the slice: x: 2, y: 2, z: 4, core: 2. Of those that a mesh axis runs over, the one named last changes fastest.
Arguments:
- tensor: float32 [256, 128, 128], P(('groups', 'row')), parts along dimension 0, may hold values from -6 to 6
- init_second: float32 [256, 512], P('groups'), parts along dimension 0, may hold values from -6 to 6
- init_third: float32 [256, 512], P('groups'), parts along dimension 0, may hold values from -6 to 6
Outputs:
- factor_first: float32 [256, 512], P(('groups', 'row')), parts along dimension 0
- factor_second: float32 [256, 512], P(('groups', 'row')), parts along dimension 0
- factor_third: float32 [256, 512], P('groups'), parts along dimension 0
- weights: float32 [1024], P('groups'), parts along dimension 0
There are 2 independent parts, one for each index of `groups`. A program takes and returns all parts, laid end to end along the dimension named above; each array names one. Nothing has to cross between parts.
All inputs are finite; a program needn't handle non-finite values.
Results may differ from a plain program's by a relative error of at most 0.0001.
Values sent between devices are 32-bit elements; how exact they have to be, the bound alone decides.
A program may use at most 128 MiB of HBM per device.

v0:
```python
import math
import jax
import jax.numpy as jnp
from jax import lax
from jax.sharding import PartitionSpec as P

HIGHEST = lax.Precision.HIGHEST
RIDGE = 0.05
EPSILON = 1e-06


def plain_gram(factor):
    return jnp.dot(factor.T, factor, precision=HIGHEST, preferred_element_type=jnp.float32)


def ridge_solve(right, first, second):
    hadamard = first * second
    shift = RIDGE * jnp.mean(jnp.diagonal(hadamard))
    system = hadamard + shift * jnp.eye(hadamard.shape[0], dtype=jnp.float32)
    lower = jnp.linalg.cholesky(system)
    return jax.scipy.linalg.cho_solve((lower, True), right.T).T


def column_scales(gram_raw):
    return jnp.sqrt(jnp.diagonal(gram_raw) + EPSILON)


def on_device(tensor, init_second, init_third):
    local_rows, second_cells, depth_cells = tensor.shape
    factor_cols = init_second.shape[1]
    devices = lax.axis_size("row")
    total_first = local_rows * devices
    gram_b0 = plain_gram(init_second) / second_cells
    gram_c0 = plain_gram(init_third) / depth_cells
    contracted = jnp.einsum("ijk,kr->ijr", tensor, init_third, precision=HIGHEST)
    right_a = jnp.einsum("ijr,jr->ir", contracted, init_second, precision=HIGHEST)
    raw_a = ridge_solve(right_a, gram_b0, gram_c0)
    gram_raw_a = lax.psum(plain_gram(raw_a), "row") / total_first
    scales_a = column_scales(gram_raw_a)
    factor_first = raw_a / scales_a
    gram_a = gram_raw_a / (scales_a[:, None] * scales_a[None, :])
    empty_product = jnp.zeros((local_rows, depth_cells, factor_cols), jnp.float32)
    segment = contracted
    right_own = lax.psum_scatter(
        jnp.einsum("ijr,ir->jr", segment, factor_first, precision=HIGHEST),
        "row",
        scatter_dimension=0,
        tiled=True,
    )
    raw_own = ridge_solve(right_own, gram_a, gram_c0)
    empty_gram = jnp.zeros((factor_cols, factor_cols), jnp.float32)
    segment = lax.all_gather(raw_own, "row", axis=0, tiled=True)
    product_raw = (empty_product, empty_gram)[0] + jnp.einsum(
        "ijk,jr->ikr", tensor, segment, precision=HIGHEST
    )
    gram_total = plain_gram(segment)
    gram_raw_b = gram_total / second_cells
    scales_b = column_scales(gram_raw_b)
    factor_second = raw_own / scales_b
    product = product_raw / scales_b
    gram_b = gram_raw_b / (scales_b[:, None] * scales_b[None, :])
    right_part = jnp.einsum("ikr,ir->kr", product, factor_first, precision=HIGHEST)
    right_c_own = lax.psum_scatter(right_part, "row", scatter_dimension=0, tiled=True)
    raw_c = lax.all_gather(ridge_solve(right_c_own, gram_a, gram_b), "row", axis=0, tiled=True)
    scales_c = jnp.sqrt(jnp.mean(raw_c * raw_c, axis=0) + EPSILON)
    factor_third = raw_c / scales_c
    weights = scales_c / math.sqrt(total_first * second_cells)
    return (factor_first, factor_second, factor_third, weights)


def solution(mesh):
    in_specs = (P(("groups", "row"), None, None), P("groups", None), P("groups", None))
    out_specs = (
        P(("groups", "row"), None),
        P(("groups", "row"), None),
        P("groups", None),
        P("groups"),
    )
    return jax.shard_map(
        on_device, mesh=mesh, in_specs=in_specs, out_specs=out_specs, check_vma=False
    )
```

profile of v0, /device:TPU:0, one launch (start us, length us, event | category | flops | bytes accessed | tf_op | source)
XLA Modules:
  0.0 632.8 jit_solution(15217960713749262886)
XLA Ops:
  7.2 2.1 convolution_multiply_fusion.1
  10.3 2.1 fusion.2
  12.4 4.7 gather_fusion
  19.9 1.5 fusion.5
  22.4 11.7 %cholesky.374 = f32[128,128]{1,0:T(8,128)S(1)} custom-call(f32[128,128]{1,0:T(8,128)S(1)} %cholesky.586), custom_call_target="Cholesky" | custom-call | tf_op jit(solution)/shard_map/jit(cholesky)/cholesky | solution.py:20
  34.1 9.8 %custom-call.43 = f32[1,128,128]{1,2,0:T(8,128)S(1)} custom-call(f32[1,128,128]{2,1,0:T(8,128)S(1)} %get-tuple-element.88), custom_call_target="InvertDiagBlocksLowerTriangular" | custom-call | tf_op jit(solution)/shard_map/jit(cholesky)/cholesky | solution.py:20
  46.6 11.7 %cholesky.393 = f32[128,128]{1,0:T(8,128)S(1)} custom-call(f32[128,128]{1,0:T(8,128)S(1)} %cholesky.590), custom_call_target="Cholesky" | custom-call | tf_op jit(solution)/shard_map/jit(cholesky)/cholesky | solution.py:20
  58.3 10.0 %custom-call.44 = f32[1,128,128]{1,2,0:T(8,128)S(1)} custom-call(f32[1,128,128]{2,1,0:T(8,128)S(1)} %get-tuple-element.85), custom_call_target="InvertDiagBlocksLowerTriangular" | custom-call | tf_op jit(solution)/shard_map/jit(cholesky)/cholesky | solution.py:20
  69.9 11.7 %cholesky.414 = f32[128,128]{1,0:T(8,128)S(1)} custom-call(f32[128,128]{1,0:T(8,128)S(1)} %cholesky.595), custom_call_target="Cholesky" | custom-call | tf_op jit(solution)/shard_map/jit(cholesky)/cholesky | solution.py:20
  82.4 9.8 %custom-call.45 = f32[1,128,128]{1,2,0:T(8,128)S(1)} custom-call(f32[1,128,128]{2,1,0:T(8,128)S(1)} %get-tuple-element.82), custom_call_target="InvertDiagBlocksLowerTriangular" | custom-call | tf_op jit(solution)/shard_map/jit(cholesky)/cholesky | solution.py:20
  93.6 11.7 %cholesky.431 = f32[128,128]{1,0:T(8,128)S(1)} custom-call(f32[128,128]{1,0:T(8,128)S(1)} %convolution_subtract_fusion.8), custom_call_target="Cholesky" | custom-call | tf_op jit(solution)/shard_map/jit(cholesky)/cholesky | solution.py:20
  110.0 8.0 %while.6 = (s32[]{:T(128)}, f32[512,512]{1,0:T(8,128)S(1)}, s32[4,2]{0,1:T(2,128)S(1)}, f32[4,128,128]{2,1,0:T(8,128)S(1)}, s32[]{:T(128)}) while((s32[]{:T(128)}, f32[512,512]{1,0:T(8,128)S(1)}, s32[4,2]{0,1:T(2,128)S(1)}, f32[4,128,128]{2,1,0:T(8,128)S(1)}, s32[]{:T(128)}) %tuple.78), condition=%wide.while_cond, body=%wide.while_body.sunk | while | flops 2 | bytes 131189 | solution.py:21
  112.6 1.4 bitcast_dynamic-update-slice_fusion.6
  118.0 39.3 %custom-call.46 = f32[4,128,128]{1,2,0:T(8,128)S(1)} custom-call(f32[4,128,128]{2,1,0:T(8,128)S(1)} %get-tuple-element.26), custom_call_target="InvertDiagBlocksLowerTriangular" | custom-call | tf_op jit(solution)/shard_map/jit(_cho_solve)/triangular_solve | solution.py:21
  157.4 3.3 multiply_reduce_fusion.1
  163.5 2.0 fusion.116
  165.7 96.7 %all-reduce.3.cloned.1.call-done = f32[512,512]{0,1:T(8,128)} async-done(((f32[512,512]{0,1:T(8,128)}), f32[512,512]{0,1:T(8,128)}) %all-reduce.3.cloned.1.call-update) | async-done | bytes 1048592 | tf_op jit(solution)/shard_map/psum | solution.py:38
  263.7 4.5 gather_fusion.1
  268.3 2.6 multiply_reduce_fusion
  270.9 1.5 fusion.39
  272.4 4.7 gather_fusion.2
  279.8 1.5 fusion.4
  281.3 11.7 %cholesky.446 = f32[128,128]{1,0:T(8,128)S(1)} custom-call(f32[128,128]{1,0:T(8,128)S(1)} %cholesky.599), custom_call_target="Cholesky" | custom-call | tf_op jit(solution)/shard_map/jit(cholesky)/cholesky | solution.py:20
  293.7 9.8 %custom-call.47 = f32[1,128,128]{1,2,0:T(8,128)S(1)} custom-call(f32[1,128,128]{2,1,0:T(8,128)S(1)} %get-tuple-element.78), custom_call_target="InvertDiagBlocksLowerTriangular" | custom-call | tf_op jit(solution)/shard_map/jit(cholesky)/cholesky | solution.py:20
  304.3 11.7 %cholesky.465 = f32[128,128]{1,0:T(8,128)S(1)} custom-call(f32[128,128]{1,0:T(8,128)S(1)} %cholesky.603), custom_call_target="Cholesky" | custom-call | tf_op jit(solution)/shard_map/jit(cholesky)/cholesky | solution.py:20
  316.7 10.0 %custom-call.48 = f32[1,128,128]{1,2,0:T(8,128)S(1)} custom-call(f32[1,128,128]{2,1,0:T(8,128)S(1)} %get-tuple-element.75), custom_call_target="InvertDiagBlocksLowerTriangular" | custom-call | tf_op jit(solution)/shard_map/jit(cholesky)/cholesky | solution.py:20
  327.3 11.7 %cholesky.486 = f32[128,128]{1,0:T(8,128)S(1)} custom-call(f32[128,128]{1,0:T(8,128)S(1)} %cholesky.608), custom_call_target="Cholesky" | custom-call | tf_op jit(solution)/shard_map/jit(cholesky)/cholesky | solution.py:20
  339.8 9.8 %custom-call.49 = f32[1,128,128]{1,2,0:T(8,128)S(1)} custom-call(f32[1,128,128]{2,1,0:T(8,128)S(1)} %get-tuple-element.72), custom_call_target="InvertDiagBlocksLowerTriangular" | custom-call | tf_op jit(solution)/shard_map/jit(cholesky)/cholesky | solution.py:20
  350.2 11.7 %cholesky.503 = f32[128,128]{1,0:T(8,128)S(1)} custom-call(f32[128,128]{1,0:T(8,128)S(1)} %convolution_subtract_fusion.7), custom_call_target="Cholesky" | custom-call | tf_op jit(solution)/shard_map/jit(cholesky)/cholesky | solution.py:20
  365.5 7.7 %while.7 = (s32[]{:T(128)}, f32[512,512]{1,0:T(8,128)S(1)}, s32[4,2]{0,1:T(2,128)S(1)}, f32[4,128,128]{2,1,0:T(8,128)S(1)}, s32[]{:T(128)}) while((s32[]{:T(128)}, f32[512,512]{1,0:T(8,128)S(1)}, s32[4,2]{0,1:T(2,128)S(1)}, f32[4,128,128]{2,1,0:T(8,128)S(1)}, s32[]{:T(128)}) %tuple.93), condition=%wide.while_cond.clone, body=%wide.while_body.clone.sunk | while | flops 2 | bytes 131189 | solution.py:21
  373.4 39.3 %custom-call.50 = f32[4,128,128]{1,2,0:T(8,128)S(1)} custom-call(f32[4,128,128]{2,1,0:T(8,128)S(1)} %get-tuple-element.27), custom_call_target="InvertDiagBlocksLowerTriangular" | custom-call | tf_op jit(solution)/shard_map/jit(_cho_solve)/triangular_solve | solution.py:21
  418.3 20.2 %all_gather.6 = f32[128,512]{1,0:T(8,128)S(1)} all-gather(f32[8,512]{1,0:T(8,128)S(1)} %maximum_bitcast_fusion), channel_id=1, replica_groups=mesh['groups'=2,'row'=16] {'row'}, dimensions={0}, use_global_device_ids=true | all-gather | bytes 278528 | tf_op jit(solution)/shard_map/all_gather | solution.py:52
  439.6 4.5 gather_fusion.3
  444.1 3.2 divide_bitcast_fusion
  447.7 4.7 gather_fusion.4
  455.1 1.5 fusion.3
  456.6 11.7 %cholesky.518 = f32[128,128]{1,0:T(8,128)S(1)} custom-call(f32[128,128]{1,0:T(8,128)S(1)} %cholesky.612), custom_call_target="Cholesky" | custom-call | tf_op jit(solution)/shard_map/jit(cholesky)/cholesky | solution.py:20
  469.0 9.8 %custom-call.51 = f32[1,128,128]{1,2,0:T(8,128)S(1)} custom-call(f32[1,128,128]{2,1,0:T(8,128)S(1)} %get-tuple-element.68), custom_call_target="InvertDiagBlocksLowerTriangular" | custom-call | tf_op jit(solution)/shard_map/jit(cholesky)/cholesky | solution.py:20
  479.6 11.7 %cholesky.537 = f32[128,128]{1,0:T(8,128)S(1)} custom-call(f32[128,128]{1,0:T(8,128)S(1)} %cholesky.616), custom_call_target="Cholesky" | custom-call | tf_op jit(solution)/shard_map/jit(cholesky)/cholesky | solution.py:20
  492.0 10.0 %custom-call.52 = f32[1,128,128]{1,2,0:T(8,128)S(1)} custom-call(f32[1,128,128]{2,1,0:T(8,128)S(1)} %get-tuple-element.65), custom_call_target="InvertDiagBlocksLowerTriangular" | custom-call | tf_op jit(solution)/shard_map/jit(cholesky)/cholesky | solution.py:20
  502.7 11.7 %cholesky.558 = f32[128,128]{1,0:T(8,128)S(1)} custom-call(f32[128,128]{1,0:T(8,128)S(1)} %cholesky.621), custom_call_target="Cholesky" | custom-call | tf_op jit(solution)/shard_map/jit(cholesky)/cholesky | solution.py:20
  515.1 9.8 %custom-call.53 = f32[1,128,128]{1,2,0:T(8,128)S(1)} custom-call(f32[1,128,128]{2,1,0:T(8,128)S(1)} %get-tuple-element.62), custom_call_target="InvertDiagBlocksLowerTriangular" | custom-call | tf_op jit(solution)/shard_map/jit(cholesky)/cholesky | solution.py:20
  525.5 11.7 %cholesky.575 = f32[128,128]{1,0:T(8,128)S(1)} custom-call(f32[128,128]{1,0:T(8,128)S(1)} %convolution_subtract_fusion.6), custom_call_target="Cholesky" | custom-call | tf_op jit(solution)/shard_map/jit(cholesky)/cholesky | solution.py:20
  537.9 6.5 %fusion = f32[512,1,128]{2,1,0:T(1,128)S(1)} fusion(f32[8,512,1]{0,2,1:T(1,128)S(1)} %copy.47, f32[8,128,512]{1,2,0:T(8,128)} %divide_bitcast_fusion), kind=kOutput, calls=%fused_computation.11 | convolution fusion | flops 6291456 | bytes 2375680 | tf_op jit(solution)/shard_map/ikr,ir->kr/dot_general | solution.py:62
  547.9 7.7 %while.8 = (s32[]{:T(128)}, f32[512,512]{1,0:T(8,128)S(1)}, s32[4,2]{0,1:T(2,128)S(1)}, f32[4,128,128]{2,1,0:T(8,128)S(1)}, s32[]{:T(128)}) while((s32[]{:T(128)}, f32[512,512]{1,0:T(8,128)S(1)}, s32[4,2]{0,1:T(2,128)S(1)}, f32[4,128,128]{2,1,0:T(8,128)S(1)}, s32[]{:T(128)}) %tuple.94), condition=%wide.while_cond.clone.1, body=%wide.while_body.clone.1.sunk | while | flops 2 | bytes 131189 | solution.py:21
  555.6 39.3 %custom-call.54 = f32[4,128,128]{1,2,0:T(8,128)S(1)} custom-call(f32[4,128,128]{2,1,0:T(8,128)S(1)} %get-tuple-element.28), custom_call_target="InvertDiagBlocksLowerTriangular" | custom-call | tf_op jit(solution)/shard_map/jit(_cho_solve)/triangular_solve | solution.py:21
  595.5 3.2 reduce-scatter.9.cloned.1.call-done
  604.4 20.2 %all_gather.7 = f32[128,512]{1,0:T(8,128)S(1)} all-gather(f32[8,512]{1,0:T(8,128)S(1)} %maximum_bitcast_fusion.1), channel_id=1, replica_groups=mesh['groups'=2,'row'=16] {'row'}, dimensions={0}, use_global_device_ids=true | all-gather | bytes 278528 | tf_op jit(solution)/shard_map/all_gather | solution.py:64
  (185 shorter events, 68.4 us)
Async XLA Ops:
  7.2 150.2 %copy-start = (f32[8,128,128]{2,1,0:T(8,128)S(1)}, f32[8,128,128]{2,1,0:T(8,128)}, u32[]{:S(2)}) copy-start(f32[8,128,128]{2,1,0:T(8,128)} %param.6) | copy-start | bytes 1572868
  7.2 255.1 %all-reduce.3.cloned.1.call-start = ((), (), s32[]{:S(2)}) async-start(), calls=%async_computation.2 | async-start | bytes 2097152 | tf_op jit(solution)/shard_map/psum | solution.py:38
  9.4 1.0 copy-start.3
  21.3 1.0 copy-start.4
  69.9 87.5 %copy-start.5 = (f32[128,512]{1,0:T(8,128)S(1)}, f32[128,512]{1,0:T(8,128)}, u32[]{:S(2)}) copy-start(f32[128,512]{1,0:T(8,128)} %param.8) | copy-start | bytes 786436
  69.9 87.5 %copy-start.6 = (f32[128,512]{1,0:T(8,128)S(1)}, f32[128,512]{1,0:T(8,128)}, u32[]{:S(2)}) copy-start(f32[128,512]{1,0:T(8,128)} %param.7) | copy-start | bytes 786436
  165.6 247.1 %reduce-scatter.7.cloned.1.call-start = ((), (), s32[]{:S(2)}) async-start(), calls=%async_computation.3 | async-start | bytes 278528 | tf_op jit(solution)/shard_map/reduce_scatter | solution.py:44
  263.6 7.3 %copy-start.1 = (f32[512,512]{0,1:T(8,128)S(1)}, f32[512,512]{0,1:T(8,128)}, u32[]{:S(2)}) copy-start(f32[512,512]{0,1:T(8,128)} %all-reduce.3.cloned.1.call-done) | copy-start | bytes 3145732
  268.2 105.0 %copy-start.7 = (f32[512,8]{0,1:T(8,128)}, f32[512,8]{0,1:T(8,128)S(1)}, u32[]{:S(2)}) copy-start(f32[512,8]{0,1:T(8,128)S(1)} %fusion.115) | copy-start | bytes 49156
  270.9 327.9 %reduce-scatter.9.cloned.1.call-start = ((), (), s32[]{:S(2)}) async-start(), calls=%async_computation.4 | async-start | bytes 278528 | tf_op jit(solution)/shard_map/reduce_scatter | solution.py:63
  444.1 3.2 copy-start.2
Sparse Core Ops, SparseCore 0:
  165.7 96.5 all-reduce.2
  271.0 55.1 reduce-scatter.6
  545.4 53.3 reduce-scatter.8
where the time goes:
time: 636 us; the launch traced here: 633 us
  other arithmetic  371 us (58%)
  waiting for transfers between devices  100 us (16%)
  local copies, waits for them, and re-layouts  53.8 us (8%)
  matrix products  43.5 us (7%)
  blocking collectives  40.4 us (6%)
  between operations  24.2 us (4%)
    another operation x44, other arithmetic, ridge_solve(): lower = jnp.linalg.cholesky(system)  237 us
    another operation x7, other arithmetic, ridge_solve(): return jax.scipy.linalg.cho_solve((lower, True), right.T).T  119 us
    psum x1, waiting for transfers between devices, on_device(): gram_raw_a = lax.psum(plain_gram(raw_a), 'row') / total_first  96.7 us
    another operation x40, local copies, waits for them, and re-layouts, ridge_solve(): return jax.scipy.linalg.cho_solve((lower, True), right.T).T  23.2 us
    all_gather x1, blocking collectives, on_device(): lax.all_gather(ridge_solve(right_c_own, gram_a, gram_b), 'row', axis=0, t...  20.2 us
    all_gather x1, blocking collectives, on_device(): segment = lax.all_gather(raw_own, 'row', axis=0, tiled=True)  20.2 us
    gather x3, local copies, waits for them, and re-layouts, ridge_solve(): shift = RIDGE * jnp.mean(jnp.diagonal(hadamard))  14.2 us
    another operation x42, matrix products, ridge_solve(): return jax.scipy.linalg.cho_solve((lower, True), right.T).T  14.1 us
  transfers between devices with their start and end apart: 3, of which 2 were waited for; matrix products, arithmetic and copies ran while one was open for 29% of the time, Pallas kernels for 0%

commit v1 on v0

--- a/solution.py
+++ b/solution.py
@@ -1,12 +1,21 @@
+import functools
 import math
 import jax
 import jax.numpy as jnp
 from jax import lax
 from jax.sharding import PartitionSpec as P
+from jax.lax import all_gather
 
 HIGHEST = lax.Precision.HIGHEST
 RIDGE = 0.05
 EPSILON = 1e-06
+
+
+def note_rounds(my_data, axis_id):
+    return all_gather(my_data, axis_id).sum(axis=0)
+
+
+stages_all_recast = functools.partial(note_rounds, axis_id="row")
 
 
 def plain_gram(factor):
@@ -35,7 +44,7 @@
     contracted = jnp.einsum("ijk,kr->ijr", tensor, init_third, precision=HIGHEST)
     right_a = jnp.einsum("ijr,jr->ir", contracted, init_second, precision=HIGHEST)
     raw_a = ridge_solve(right_a, gram_b0, gram_c0)
-    gram_raw_a = lax.psum(plain_gram(raw_a), "row") / total_first
+    gram_raw_a = stages_all_recast(plain_gram(raw_a)) / total_first
     scales_a = column_scales(gram_raw_a)
     factor_first = raw_a / scales_a
     gram_a = gram_raw_a / (scales_a[:, None] * scales_a[None, :])

time: 636 us -> 685 us (1.077)
  waiting for transfers between devices: 100 us -> 129 us
  other arithmetic: 371 us -> 380 us
  local copies, waits for them, and re-layouts: 53.8 us -> 61.3 us
    all_gather x0 -> x1, waiting for transfers between devices: none -> 129 us  [note_rounds(): return all_gather(my_data, axis_id).sum(axis=0)]
    psum x1 -> x0, waiting for transfers between devices: 96.7 us -> none  [on_device(): gram_raw_a = lax.psum(plain_gram(raw_a), 'row') / total_first]
    reduce_sum x0 -> x1, other arithmetic: none -> 7.95 us  [note_rounds(): return all_gather(my_data, axis_id).sum(axis=0)]
  transfers between devices with their start and end apart: 3 -> 3, of which waited for: 2 -> 2; matrix products, arithmetic and copies ran while one was open for 29% -> 28% of each run, Pallas kernels for 0% -> 0%
where the time goes in v1:
time: 685 us; the launch traced here: 681 us
  other arithmetic  380 us (55%)
  waiting for transfers between devices  129 us (19%)
  local copies, waits for them, and re-layouts  61.3 us (9%)
  matrix products  47.2 us (7%)
  blocking collectives  38.3 us (6%)
  between operations  24.5 us (4%)
    another operation x44, other arithmetic, ridge_solve(): lower = jnp.linalg.cholesky(system)  237 us
    all_gather x1, waiting for transfers between devices, note_rounds(): return all_gather(my_data, axis_id).sum(axis=0)  129 us
    another operation x7, other arithmetic, ridge_solve(): return jax.scipy.linalg.cho_solve((lower, True), right.T).T  120 us
    another operation x40, local copies, waits for them, and re-layouts, ridge_solve(): return jax.scipy.linalg.cho_solve((lower, True), right.T).T  27.5 us
    all_gather x1, blocking collectives, on_device(): segment = lax.all_gather(raw_own, 'row', axis=0, tiled=True)  20.1 us
    all_gather x1, blocking collectives, on_device(): lax.all_gather(ridge_solve(right_c_own, gram_a, gram_b), 'row', axis=0, t...  18.2 us
    another operation x42, matrix products, ridge_solve(): return jax.scipy.linalg.cho_solve((lower, True), right.T).T  17.4 us
    gather x3, local copies, waits for them, and re-layouts, ridge_solve(): shift = RIDGE * jnp.mean(jnp.diagonal(hadamard))  14.7 us
  transfers between devices with their start and end apart: 3, of which 2 were waited for; matrix products, arithmetic and copies ran while one was open for 28% of the time, Pallas kernels for 0%

profile of v1, /device:TPU:0, one launch (start us, length us, event | category | flops | bytes accessed | tf_op | source)
XLA Modules:
  0.0 681.4 jit_solution(14470539792063403051)
XLA Ops:
  7.2 2.1 convolution_multiply_fusion.1
  10.4 2.1 fusion.2
  12.5 5.1 gather_fusion
  21.7 11.7 %cholesky.374 = f32[128,128]{1,0:T(8,128)S(1)} custom-call(f32[128,128]{1,0:T(8,128)S(1)} %cholesky.586), custom_call_target="Cholesky" | custom-call | tf_op jit(solution)/shard_map/jit(cholesky)/cholesky | solution.py:29
  33.5 9.8 %custom-call.43 = f32[1,128,128]{1,2,0:T(8,128)S(1)} custom-call(f32[1,128,128]{2,1,0:T(8,128)S(1)} %get-tuple-element.88), custom_call_target="InvertDiagBlocksLowerTriangular" | custom-call | tf_op jit(solution)/shard_map/jit(cholesky)/cholesky | solution.py:29
  44.1 11.7 %cholesky.393 = f32[128,128]{1,0:T(8,128)S(1)} custom-call(f32[128,128]{1,0:T(8,128)S(1)} %cholesky.590), custom_call_target="Cholesky" | custom-call | tf_op jit(solution)/shard_map/jit(cholesky)/cholesky | solution.py:29
  55.8 10.0 %custom-call.44 = f32[1,128,128]{1,2,0:T(8,128)S(1)} custom-call(f32[1,128,128]{2,1,0:T(8,128)S(1)} %get-tuple-element.85), custom_call_target="InvertDiagBlocksLowerTriangular" | custom-call | tf_op jit(solution)/shard_map/jit(cholesky)/cholesky | solution.py:29
  66.5 11.7 %cholesky.414 = f32[128,128]{1,0:T(8,128)S(1)} custom-call(f32[128,128]{1,0:T(8,128)S(1)} %cholesky.595), custom_call_target="Cholesky" | custom-call | tf_op jit(solution)/shard_map/jit(cholesky)/cholesky | solution.py:29
  79.0 9.8 %custom-call.45 = f32[1,128,128]{1,2,0:T(8,128)S(1)} custom-call(f32[1,128,128]{2,1,0:T(8,128)S(1)} %get-tuple-element.82), custom_call_target="InvertDiagBlocksLowerTriangular" | custom-call | tf_op jit(solution)/shard_map/jit(cholesky)/cholesky | solution.py:29
  89.4 11.7 %cholesky.431 = f32[128,128]{1,0:T(8,128)S(1)} custom-call(f32[128,128]{1,0:T(8,128)S(1)} %convolution_subtract_fusion.8), custom_call_target="Cholesky" | custom-call | tf_op jit(solution)/shard_map/jit(cholesky)/cholesky | solution.py:29
  105.3 8.0 %while.6 = (s32[]{:T(128)}, f32[512,512]{1,0:T(8,128)S(1)}, s32[4,2]{0,1:T(2,128)S(1)}, f32[4,128,128]{2,1,0:T(8,128)S(1)}, s32[]{:T(128)}) while((s32[]{:T(128)}, f32[512,512]{1,0:T(8,128)S(1)}, s32[4,2]{0,1:T(2,128)S(1)}, f32[4,128,128]{2,1,0:T(8,128)S(1)}, s32[]{:T(128)}) %tuple.78), condition=%wide.while_cond, body=%wide.while_body.sunk | while | flops 2 | bytes 131181 | solution.py:30
  113.3 39.3 %custom-call.46 = f32[4,128,128]{1,2,0:T(8,128)S(1)} custom-call(f32[4,128,128]{2,1,0:T(8,128)S(1)} %get-tuple-element.26), custom_call_target="InvertDiagBlocksLowerTriangular" | custom-call | tf_op jit(solution)/shard_map/jit(_cho_solve)/triangular_solve | solution.py:30
  152.7 3.3 multiply_reduce_fusion.1
  158.9 2.1 fusion.116
  161.0 129.3 %all-gather.3.cloned.1.call-done = f32[8192,512]{1,0:T(8,128)} async-done(((f32[512,512]{1,0:T(8,128)}), f32[8192,512]{1,0:T(8,128)}) %all-gather.3.cloned.1.call-update) | async-done | bytes 16777232 | tf_op jit(solution)/shard_map/all_gather | solution.py:15
  290.3 8.0 %reduce_sum.46 = f32[512,512]{1,0:T(8,128)S(1)} reduce(f32[16,512,512]{2,1,0:T(8,128)} %bitcast.223, f32[]{:T(128)} %constant.145.clone.1), dimensions={0}, to_apply=%region_9.12 | reduce | flops 3932160 | bytes 17825796 | tf_op jit(solution)/shard_map/reduce_sum | solution.py:15
  298.7 4.5 gather_fusion.1
  304.8 5.0 gather_fusion.2
  312.1 2.6 copy.23
  317.2 11.7 %cholesky.446 = f32[128,128]{1,0:T(8,128)S(1)} custom-call(f32[128,128]{1,0:T(8,128)S(1)} %cholesky.599), custom_call_target="Cholesky" | custom-call | tf_op jit(solution)/shard_map/jit(cholesky)/cholesky | solution.py:29
  329.0 9.8 %custom-call.47 = f32[1,128,128]{1,2,0:T(8,128)S(1)} custom-call(f32[1,128,128]{2,1,0:T(8,128)S(1)} %get-tuple-element.78), custom_call_target="InvertDiagBlocksLowerTriangular" | custom-call | tf_op jit(solution)/shard_map/jit(cholesky)/cholesky | solution.py:29
  341.4 11.7 %cholesky.465 = f32[128,128]{1,0:T(8,128)S(1)} custom-call(f32[128,128]{1,0:T(8,128)S(1)} %cholesky.603), custom_call_target="Cholesky" | custom-call | tf_op jit(solution)/shard_map/jit(cholesky)/cholesky | solution.py:29
  354.4 10.0 %custom-call.48 = f32[1,128,128]{1,2,0:T(8,128)S(1)} custom-call(f32[1,128,128]{2,1,0:T(8,128)S(1)} %get-tuple-element.75), custom_call_target="InvertDiagBlocksLowerTriangular" | custom-call | tf_op jit(solution)/shard_map/jit(cholesky)/cholesky | solution.py:29
  366.0 11.7 %cholesky.486 = f32[128,128]{1,0:T(8,128)S(1)} custom-call(f32[128,128]{1,0:T(8,128)S(1)} %cholesky.608), custom_call_target="Cholesky" | custom-call | tf_op jit(solution)/shard_map/jit(cholesky)/cholesky | solution.py:29
  378.4 9.8 %custom-call.49 = f32[1,128,128]{1,2,0:T(8,128)S(1)} custom-call(f32[1,128,128]{2,1,0:T(8,128)S(1)} %get-tuple-element.72), custom_call_target="InvertDiagBlocksLowerTriangular" | custom-call | tf_op jit(solution)/shard_map/jit(cholesky)/cholesky | solution.py:29
  389.7 11.7 %cholesky.503 = f32[128,128]{1,0:T(8,128)S(1)} custom-call(f32[128,128]{1,0:T(8,128)S(1)} %convolution_subtract_fusion.7), custom_call_target="Cholesky" | custom-call | tf_op jit(solution)/shard_map/jit(cholesky)/cholesky | solution.py:29
  402.1 3.0 multiply_reduce_fusion
  408.8 11.3 %while.7 = (s32[]{:T(128)}, f32[512,512]{1,0:T(8,128)}, s32[4,2]{0,1:T(2,128)S(1)}, f32[4,128,128]{2,1,0:T(8,128)S(1)}, s32[]{:T(128)}) while((s32[]{:T(128)}, f32[512,512]{1,0:T(8,128)}, s32[4,2]{0,1:T(2,128)S(1)}, f32[4,128,128]{2,1,0:T(8,128)S(1)}, s32[]{:T(128)}) %tuple.93), condition=%wide.while_cond.clone, body=%wide.while_body.clone.sunk | while | flops 2 | bytes 131181 | solution.py:30
  409.5 2.2 bitcast_dynamic-update-slice_fusion.7
  412.3 2.2 bitcast_dynamic-update-slice_fusion.7
  415.1 2.2 bitcast_dynamic-update-slice_fusion.7
  418.0 2.1 bitcast_dynamic-update-slice_fusion.7
  420.1 39.3 %custom-call.50 = f32[4,128,128]{1,2,0:T(8,128)S(1)} custom-call(f32[4,128,128]{2,1,0:T(8,128)S(1)} %get-tuple-element.27), custom_call_target="InvertDiagBlocksLowerTriangular" | custom-call | tf_op jit(solution)/shard_map/jit(_cho_solve)/triangular_solve | solution.py:30
  468.6 20.1 %all_gather.14 = f32[128,512]{1,0:T(8,128)S(1)} all-gather(f32[8,512]{1,0:T(8,128)S(1)} %maximum_bitcast_fusion), channel_id=1, replica_groups=mesh['groups'=2,'row'=16] {'row'}, dimensions={0}, use_global_device_ids=true | all-gather | bytes 278528 | tf_op jit(solution)/shard_map/all_gather | solution.py:61
  489.8 4.5 gather_fusion.3
  494.3 1.9 divide_bitcast_fusion
  497.8 4.6 fusion
  503.2 4.7 gather_fusion.4
  513.2 11.7 %cholesky.518 = f32[128,128]{1,0:T(8,128)S(1)} custom-call(f32[128,128]{1,0:T(8,128)S(1)} %cholesky.612), custom_call_target="Cholesky" | custom-call | tf_op jit(solution)/shard_map/jit(cholesky)/cholesky | solution.py:29
  525.0 9.8 %custom-call.51 = f32[1,128,128]{1,2,0:T(8,128)S(1)} custom-call(f32[1,128,128]{2,1,0:T(8,128)S(1)} %get-tuple-element.68), custom_call_target="InvertDiagBlocksLowerTriangular" | custom-call | tf_op jit(solution)/shard_map/jit(cholesky)/cholesky | solution.py:29
  537.4 11.7 %cholesky.537 = f32[128,128]{1,0:T(8,128)S(1)} custom-call(f32[128,128]{1,0:T(8,128)S(1)} %cholesky.616), custom_call_target="Cholesky" | custom-call | tf_op jit(solution)/shard_map/jit(cholesky)/cholesky | solution.py:29
  550.4 10.0 %custom-call.52 = f32[1,128,128]{1,2,0:T(8,128)S(1)} custom-call(f32[1,128,128]{2,1,0:T(8,128)S(1)} %get-tuple-element.65), custom_call_target="InvertDiagBlocksLowerTriangular" | custom-call | tf_op jit(solution)/shard_map/jit(cholesky)/cholesky | solution.py:29
  562.0 11.7 %cholesky.558 = f32[128,128]{1,0:T(8,128)S(1)} custom-call(f32[128,128]{1,0:T(8,128)S(1)} %cholesky.621), custom_call_target="Cholesky" | custom-call | tf_op jit(solution)/shard_map/jit(cholesky)/cholesky | solution.py:29
  574.4 9.8 %custom-call.53 = f32[1,128,128]{1,2,0:T(8,128)S(1)} custom-call(f32[1,128,128]{2,1,0:T(8,128)S(1)} %get-tuple-element.62), custom_call_target="InvertDiagBlocksLowerTriangular" | custom-call | tf_op jit(solution)/shard_map/jit(cholesky)/cholesky | solution.py:29
  585.6 11.7 %cholesky.575 = f32[128,128]{1,0:T(8,128)S(1)} custom-call(f32[128,128]{1,0:T(8,128)S(1)} %convolution_subtract_fusion.6), custom_call_target="Cholesky" | custom-call | tf_op jit(solution)/shard_map/jit(cholesky)/cholesky | solution.py:29
  601.0 8.5 %while.8 = (s32[]{:T(128)}, f32[512,512]{1,0:T(8,128)S(1)}, s32[4,2]{0,1:T(2,128)S(1)}, f32[4,128,128]{2,1,0:T(8,128)S(1)}, s32[]{:T(128)}) while((s32[]{:T(128)}, f32[512,512]{1,0:T(8,128)S(1)}, s32[4,2]{0,1:T(2,128)S(1)}, f32[4,128,128]{2,1,0:T(8,128)S(1)}, s32[]{:T(128)}) %tuple.94), condition=%wide.while_cond.clone.1, body=%wide.while_body.clone.1.sunk | while | flops 2 | bytes 131181 | solution.py:30
  609.5 39.3 %custom-call.54 = f32[4,128,128]{1,2,0:T(8,128)S(1)} custom-call(f32[4,128,128]{2,1,0:T(8,128)S(1)} %get-tuple-element.28), custom_call_target="InvertDiagBlocksLowerTriangular" | custom-call | tf_op jit(solution)/shard_map/jit(_cho_solve)/triangular_solve | solution.py:30
  655.1 18.2 %all_gather.15 = f32[128,512]{1,0:T(8,128)S(1)} all-gather(f32[8,512]{1,0:T(8,128)S(1)} %maximum_bitcast_fusion.1), channel_id=1, replica_groups=mesh['groups'=2,'row'=16] {'row'}, dimensions={0}, use_global_device_ids=true | all-gather | bytes 278528 | tf_op jit(solution)/shard_map/all_gather | solution.py:73
  (187 shorter events, 79.9 us)
Async XLA Ops:
  7.2 145.5 %copy-start = (f32[8,128,128]{2,1,0:T(8,128)S(1)}, f32[8,128,128]{2,1,0:T(8,128)}, u32[]{:S(2)}) copy-start(f32[8,128,128]{2,1,0:T(8,128)} %param.6) | copy-start | bytes 1572868
  7.2 283.1 %all-gather.3.cloned.1.call-start = ((), (), s32[]{:S(2)}) async-start(), calls=%async_computation.2 | async-start | bytes 17825792 | tf_op jit(solution)/shard_map/all_gather | solution.py:15
  9.4 1.0 copy-start.2
  66.5 86.2 %copy-start.5 = (f32[128,512]{1,0:T(8,128)S(1)}, f32[128,512]{1,0:T(8,128)}, u32[]{:S(2)}) copy-start(f32[128,512]{1,0:T(8,128)} %param.8) | copy-start | bytes 786436
  66.5 86.2 %copy-start.6 = (f32[128,512]{1,0:T(8,128)S(1)}, f32[128,512]{1,0:T(8,128)}, u32[]{:S(2)}) copy-start(f32[128,512]{1,0:T(8,128)} %param.7) | copy-start | bytes 786436
  161.0 298.7 %reduce-scatter.7.cloned.1.call-start = ((), (), s32[]{:S(2)}) async-start(), calls=%async_computation.3 | async-start | bytes 278528 | tf_op jit(solution)/shard_map/reduce_scatter | solution.py:53
  304.8 154.7 %copy-start.7 = (f32[512,8]{0,1:T(8,128)}, f32[512,8]{0,1:T(8,128)S(1)}, u32[]{:S(2)}) copy-start(f32[512,8]{0,1:T(8,128)S(1)} %fusion.115) | copy-start | bytes 49156
  316.2 1.0 copy-start.3
  405.1 244.3 %reduce-scatter.9.cloned.1.call-start = ((), (), s32[]{:S(2)}) async-start(), calls=%async_computation.4 | async-start | bytes 278528 | tf_op jit(solution)/shard_map/reduce_scatter | solution.py:72
  489.7 4.6 copy-start.1
  512.2 1.0 copy-start.4
Sparse Core Ops, SparseCore 0:
  161.1 129.1 all-gather.2
  405.3 54.3 reduce-scatter.6
  503.4 53.3 reduce-scatter.8
